TPU v7x, 32 devices: a whole 2x2x4 slice. The times are simulated.
32 devices in a mesh: groups: 2 (over y), tm: 4 (over z), head: 2 (over x), batch: 2 (over core).
Axes of the slice: x: 2, y: 2, z: 4, core: 2. Of those that a mesh axis runs over, the one named last changes fastest.
Arguments:
- u_input: bfloat16 [4, 1024, 1536], P(('groups', 'batch'), 'tm'), parts along dimension 0, may hold values from -6 to 6
- head_values: bfloat16 [4, 1024, 3072], P(('groups', 'batch'), 'tm', 'head'), parts along dimension 0, may hold values from -6 to 6
- grad_output: bfloat16 [4, 1024, 3072], P(('groups', 'batch'), 'tm', 'head'), parts along dimension 0, may hold values from -6 to 6
- w_bc: bfloat16 [1536, 256], replicated, may hold values from -0.15625 to 0.15625
- w_dt: bfloat16 [1536, 48], P(None, 'head'), may hold values from -0.15625 to 0.15625
- dt_bias: float32 [48], P('head'), may hold values from -1.5 to 0.5
- a_log: float32 [48], P('head'), as said below
Outputs:
- grad_input: bfloat16 [4, 1024, 1536], P(('groups', 'batch'), 'tm'), parts along dimension 0
- grad_values: bfloat16 [4, 1024, 3072], P(('groups', 'batch'), 'tm', 'head'), parts along dimension 0
- grad_w_bc: float32 [3072, 256], P(('groups', 'tm', 'batch')), parts along dimension 0
- grad_w_dt: float32 [3072, 48], P('groups', 'head'), parts along dimension 0
- grad_dt_bias: float32 [96], P(('groups', 'head')), parts along dimension 0
- grad_a_log: float32 [96], P(('groups', 'head')), parts along dimension 0
There are 2 independent parts, one for each index of `groups`. A program takes and returns all parts, laid end to end along the dimension named above; an argument that names none is the same for every part. Nothing has to cross between parts.
Inputs may be any that keep to these rules, and one draw needn't show every extreme that they name: a_log lies between log(0.3 / 1024) and log(0.08).
All inputs are finite; a program needn't handle non-finite values.
Results may differ from a plain program's by a relative error of at most 0.0059.
Values may be sent and summed in bfloat16 or wider, within the bound.
A program may use at most 64 MiB of HBM per device.

v0:
```python
import jax
import jax.numpy as jnp
from jax import lax
from jax.sharding import PartitionSpec as P


def prefix(shard, axis, combine, identity, reverse):
    length, place = (lax.axis_size(axis), lax.axis_index(axis))
    everything = jax.tree.map(lambda part: lax.all_gather(part, axis), shard)
    start = jax.tree.map(
        lambda part, zero: jnp.broadcast_to(jnp.asarray(zero, part.dtype), part.shape),
        shard,
        identity,
    )

    def turn(k, before):
        at = length - 1 - k if reverse else k
        reached = at > place if reverse else at < place
        new = combine(before, jax.tree.map(lambda part: part[at], everything))
        return jax.tree.map(lambda a, b: jnp.where(reached, a, b), new, before)

    return lax.fori_loop(0, length, turn, start)


def span_core(b_rows, c_rows, time_step, values_in, rate, state_in):
    highest = lax.Precision.HIGHEST
    log_decay = jnp.cumsum(time_step * rate[None, :], axis=0)
    length_t = time_step.shape[0]
    causal = jnp.arange(length_t)[:, None] >= jnp.arange(length_t)[None, :]
    differ = log_decay.T[:, :, None] - log_decay.T[:, None, :]
    decay = jnp.exp(jnp.where(causal[None], differ, -jnp.inf))
    scores = jnp.dot(c_rows, b_rows.T, precision=highest)
    mixing = decay * scores[None] * time_step.T[:, None, :]
    inner = jnp.einsum("hts,shp->thp", mixing, values_in, precision=highest)
    carried = jnp.exp(log_decay)[:, :, None] * jnp.einsum(
        "tn,hpn->thp", c_rows, state_in, precision=highest
    )
    output = inner + carried
    tail_w = jnp.exp(log_decay[-1][None, :] - log_decay) * time_step
    final = jnp.exp(log_decay[-1])[:, None, None] * state_in + jnp.einsum(
        "sh,shp,sn->hpn", tail_w, values_in, b_rows, precision=highest
    )
    return (output, final)


def combine_maps(earlier, later):
    return (earlier[0] * later[0], later[0][..., None, None] * earlier[1] + later[1])


def on_device(u_input, head_values, grad_output, w_bc, w_dt, dt_bias, a_log):
    highest = lax.Precision.HIGHEST
    seq_count, token_count, width = u_input.shape
    heads = w_dt.shape[1]
    state_size = w_bc.shape[1] // 2
    head_size = head_values.shape[2] // heads
    rate = -jnp.exp(a_log)
    flat = u_input.reshape(seq_count * token_count, width)
    proj = jnp.dot(flat, w_bc, preferred_element_type=jnp.float32).astype(jnp.bfloat16)
    pre = jnp.dot(flat, w_dt, preferred_element_type=jnp.float32) + dt_bias[None, :]
    delta = jax.nn.softplus(pre).reshape(seq_count, token_count, heads)
    b_all = proj[:, :state_size].astype(jnp.float32).reshape(seq_count, token_count, state_size)
    c_all = proj[:, state_size:].astype(jnp.float32).reshape(seq_count, token_count, state_size)
    values_all = head_values.astype(jnp.float32).reshape(seq_count, token_count, heads, head_size)
    cotangent = grad_output.astype(jnp.float32).reshape(seq_count, token_count, heads, head_size)

    def summarize(b_rows, c_rows, time_step, values_in, grads_in):
        log_decay = jnp.cumsum(time_step * rate[None, :], axis=0)
        tail_w = jnp.exp(log_decay[-1][None, :] - log_decay) * time_step
        own_state = jnp.einsum("sh,shp,sn->hpn", tail_w, values_in, b_rows, precision=highest)
        pulled = jnp.einsum(
            "th,thp,tn->hpn", jnp.exp(log_decay), grads_in, c_rows, precision=highest
        )
        return (jnp.exp(log_decay[-1]), own_state, pulled)

    decays, own_states, pulls = jax.vmap(summarize)(b_all, c_all, delta, values_all, cotangent)
    unit = (jnp.ones_like(decays), jnp.zeros_like(own_states))
    incoming = prefix((decays, own_states), "tm", combine_maps, unit, False)[1]
    outgoing = prefix((decays, pulls), "tm", combine_maps, unit, True)[1]

    def backward_one(b_rows, c_rows, time_step, values_in, grads_in, state_in, state_grad):
        _, pull_back = jax.vjp(span_core, b_rows, c_rows, time_step, values_in, rate, state_in)
        return pull_back((grads_in, state_grad))

    g_b, g_c, g_delta, g_x, g_rate, _ = jax.vmap(backward_one)(
        b_all, c_all, delta, values_all, cotangent, incoming, outgoing
    )
    partial_proj = jnp.concatenate([g_b, g_c], axis=-1).reshape(
        seq_count * token_count, 2 * state_size
    )
    grad_proj = lax.psum(partial_proj, "head").astype(jnp.bfloat16)
    grad_pre = g_delta.reshape(seq_count * token_count, heads) * jax.nn.sigmoid(pre)
    grad_pre_b = grad_pre.astype(jnp.bfloat16)
    from_bc = jnp.dot(grad_proj, w_bc.T, preferred_element_type=jnp.float32)
    all_pre, all_w_dt = (
        lax.all_gather(grad_pre_b, "head", axis=1, tiled=True),
        lax.all_gather(w_dt, "head", axis=1, tiled=True),
    )
    grad_input = from_bc + jnp.dot(all_pre, all_w_dt.T, preferred_element_type=jnp.float32)
    grad_input = grad_input.astype(jnp.bfloat16).reshape(seq_count, token_count, width)
    grad_values = g_x.reshape(seq_count, token_count, heads * head_size).astype(jnp.bfloat16)
    local_w_dt = jnp.einsum("td,th->dh", flat, grad_pre_b, preferred_element_type=jnp.float32)
    grad_w_dt, grad_dt_bias, grad_a_log = lax.psum(
        (local_w_dt, jnp.sum(grad_pre, axis=0), jnp.sum(g_rate, axis=0) * rate), ("tm", "batch")
    )
    local_w_bc = jnp.einsum("td,tk->dk", flat, grad_proj, preferred_element_type=jnp.float32)
    grad_w_bc = lax.psum_scatter(local_w_bc, ("tm", "batch"), scatter_dimension=0, tiled=True)
    return (grad_input, grad_values, grad_w_bc, grad_w_dt, grad_dt_bias, grad_a_log)


def solution(mesh):
    return jax.shard_map(
        on_device,
        mesh=mesh,
        in_specs=(
            P(("groups", "batch"), "tm", None),
            P(("groups", "batch"), "tm", "head"),
            P(("groups", "batch"), "tm", "head"),
            P(),
            P(None, "head"),
            P("head"),
            P("head"),
        ),
        out_specs=(
            P(("groups", "batch"), "tm", None),
            P(("groups", "batch"), "tm", "head"),
            P(("groups", "tm", "batch"), None),
            P("groups", "head"),
            P(("groups", "head")),
            P(("groups", "head")),
        ),
        check_vma=False,
    )
```

profile of v0, /device:TPU:0, one launch (start us, length us, event | category | flops | bytes accessed | tf_op | source)
XLA Modules:
  0.0 287.1 jit_solution(3803811651553812673)
XLA Ops:
  13.4 1.8 fusion.20
  16.7 12.8 %all_gather.24 = f32[4,1,24]{2,1,0:T(1,128)} all-gather(f32[1,1,24]{2,1,0:T(1,128)S(1)} %get-tuple-element.385), channel_id=1, replica_groups=mesh['groups'=2,'tm'=4,'head'=2,'batch'=2] {'tm'}, dimensions={0}, use_global_device_ids=true | all-gather | bytes 480 | tf_op jit(solution)/shard_map/all_gather | solution.py:9
  29.5 52.0 %all-gather.5.cloned.1.call-done = f32[96,64,128]{2,1,0:T(8,128)} async-done(((f32[24,64,128]{2,1,0:T(8,128)}), f32[96,64,128]{2,1,0:T(8,128)}) %all-gather.5.cloned.1.call-update) | async-done | bytes 3145744 | tf_op jit(solution)/shard_map/all_gather | solution.py:9
  81.6 7.8 %while.30 = (s32[]{:T(128)}, f32[1,24,64,128]{3,2,1,0:T(8,128)S(1)}, s32[]{:T(128)}, f32[4,1,24]{2,1,0:T(1,128)}, f32[4,1,24,64,128]{4,3,2,1,0:T(8,128)}, /*index=5*/s32[]{:T(128)}, s32[]{:T(128)}, s32[]{:T(128)}, s32[]{:T(128)}) while((s32[]{:T(128)}, f32[1,24,64,128]{3,2,1,0:T(8,128)S(1)}, s32[]{:T(128)}, f32[4,1,24]{2,1,0:T(1,128)}, ...), condition=%wide.region_3.4_spmd.clone, body=%wide.region_2.3_spmd.clone.sunk | while | flops 786440 | bytes 2359751 | solution.py:22
  89.4 2.5 fusion.18
  91.9 1.5 copy.111
  93.4 2.2 fusion.61
  95.6 1.6 copy.90
  97.2 2.5 fusion.16
  101.3 2.0 bitcast_multiply_fusion.1
  104.0 1.6 copy.112
  105.6 1.6 copy.95
  108.2 6.4 %fusion.7 = (f32[24,256]{1,0:T(8,128)}, f32[24,256]{1,0:T(8,128)}, f32[24,256]{1,0:T(8,128)}, f32[256,256]{1,0:T(8,128)}) fusion(f32[256,256]{1,0:T(8,128)S(1)} %fusion.53, f32[24,256]{1,0:T(8,128)} %copy.95, f32[24,256]{1,0:T(8,128)S(1)} %bitcast_add_fusion.8, pred[256,256]{1,0:T(8,128)(4,1)S(1)} %iota_compare_fusion, ...), kind=kOutput, calls=%fused_computation.14 | convolution fusion | flops 221689856 | bytes 2285568 | tf_op jit(solution)/shard_map/vmap(transpose(jvp(hts,shp->thp)))/dot_general | solution.py:34
  114.6 1.5 copy.100
  116.1 1.5 copy.99
  117.6 1.5 copy.97
  120.3 3.3 %fusion.25 = f32[1,256,128]{1,2,0:T(8,128)} fusion(f32[1,256,128]{1,2,0:T(8,128)S(1)} %convolution_bitcast_fusion.3, bf16[256,24,64]{0,2,1:T(8,128)(2,1)} %bitcast.249, f32[1,24,64,128]{3,2,1,0:T(8,128)S(1)} %get-tuple-element.232, f32[256,24]{0,1:T(8,128)} %copy.90), kind=kOutput, calls=%fused_computation.42 | convolution fusion | flops 604798976 | bytes 1859584 | tf_op jit(solution)/shard_map/vmap(transpose(jvp(sh,shp,sn->hpn)))/dot_general | solution.py:40
  123.6 38.5 %all-gather.7.cloned.1.call-done = f32[96,64,128]{2,1,0:T(8,128)} async-done(((f32[24,64,128]{2,1,0:T(8,128)}), f32[96,64,128]{2,1,0:T(8,128)}) %all-gather.7.cloned.1.call-update) | async-done | bytes 3145744 | tf_op jit(solution)/shard_map/all_gather | solution.py:9
  162.1 7.8 %while.31 = (s32[]{:T(128)}, f32[1,24,64,128]{3,2,1,0:T(8,128)S(1)}, s32[]{:T(128)}, f32[4,1,24]{2,1,0:T(1,128)}, f32[4,1,24,64,128]{4,3,2,1,0:T(8,128)}, /*index=5*/s32[]{:T(128)}, s32[]{:T(128)}) while((s32[]{:T(128)}, f32[1,24,64,128]{3,2,1,0:T(8,128)S(1)}, s32[]{:T(128)}, f32[4,1,24]{2,1,0:T(1,128)}, ...), condition=%wide.region_6.7_spmd.clone, body=%wide.region_5.6_spmd.clone.sunk | while | flops 786436 | bytes 2359689 | solution.py:22
  171.4 2.5 reduce-window.16
  174.1 2.9 %convolution_bitcast_fusion.2 = f32[256,128]{0,1:T(8,128)S(1)} fusion(f32[256,24,64]{0,2,1:T(8,128)} %bitcast.250, f32[1,24,64,128]{3,2,1,0:T(8,128)S(1)} %get-tuple-element.233), kind=kOutput, calls=%fused_computation.40 | convolution fusion | flops 603979776 | bytes 2490368 | tf_op jit(solution)/shard_map/vmap(transpose(jvp(tn,hpn->thp)))/dot_general | solution.py:35
  177.4 11.5 %all-reduce.7 = bf16[256,256]{0,1:T(8,128)(2,1)S(1)} all-reduce(f32[256,256]{0,1:T(8,128)S(1)} %maximum_bitcast_fusion), channel_id=1, replica_groups=mesh['groups'=2,'tm'=4,'head'=2,'batch'=2] {'head'}, use_global_device_ids=true, to_apply=%region_7.8 | all-reduce | flops 65536 | bytes 393216 | tf_op jit(solution)/shard_map/psum | solution.py:90
  190.5 1.5 convolution_bitcast_fusion
  192.0 3.0 %copy.113 = f32[1536,256]{1,0:T(8,128)} copy(f32[1536,256]{0,1:T(8,128)} %convolution_bitcast_fusion) | data formatting | bytes 3145728
  195.9 5.0 %all_gather.30 = bf16[1536,48]{0,1:T(8,128)(2,1)S(1)} all-gather(bf16[1536,24]{0,1:T(8,128)(2,1)S(1)} %copy-done.12), channel_id=1, replica_groups=mesh['groups'=2,'tm'=4,'head'=2,'batch'=2] {'head'}, dimensions={1}, use_global_device_ids=true | all-gather | bytes 221184 | tf_op jit(solution)/shard_map/all_gather | solution.py:96
  201.0 6.0 %fusion.19 = bf16[1,256,24,64]{1,3,2,0:T(8,128)(2,1)} fusion(f32[24,64,256]{2,1,0:T(8,128)} %get-tuple-element.387, bf16[24,64,256]{2,1,0:T(8,128)(2,1)S(1)} %bitcast.245, f32[256,256]{1,0:T(8,128)S(1)} %copy-done.14, f32[24,256]{1,0:T(8,128)S(1)} %copy-done.19, f32[24,256]{1,0:T(8,128)S(1)} %copy-done.21, pred[256,256]{1,0:T(8,128)(4,1)S(1)} %copy-done.18, ...), kind=kOutput, calls=%fused_computation.32 | convolution fusion | flops 1215430656 | bytes 3547136 | tf_op jit(solution)/shard_map/vmap(transpose(jvp(hts,shp->thp)))/dot_general | solution.py:34
  207.0 2.4 copy.104
  209.6 14.1 %all-reduce.2 = (f32[24]{0:T(128)}, f32[24]{0:T(128)}) all-reduce(f32[24]{0:T(128)S(1)} %copy-done.25, f32[24]{0:T(128)S(1)} %fusion.63), channel_id=1, replica_groups=mesh['groups'=2,'tm'=4,'head'=2,'batch'=2] {'tm','batch'}, use_global_device_ids=true, to_apply=%region_19.20 | all-reduce | flops 48 | bytes 384 | tf_op jit(solution)/shard_map/psum | solution.py:102
  223.7 4.4 %all_gather.29 = bf16[256,48]{0,1:T(8,128)(2,1)S(1)} all-gather(bf16[256,24]{0,1:T(8,128)(2,1)S(1)} %copy.103), channel_id=1, replica_groups=mesh['groups'=2,'tm'=4,'head'=2,'batch'=2] {'head'}, dimensions={1}, use_global_device_ids=true | all-gather | bytes 36864 | tf_op jit(solution)/shard_map/all_gather | solution.py:95
  229.8 10.8 %all-reduce.6.cloned.1.call-done = f32[1536,24]{0,1:T(8,128)} async-done(((f32[1536,24]{0,1:T(8,128)}), f32[1536,24]{0,1:T(8,128)}) %all-reduce.6.cloned.1.call-update) | async-done | bytes 147472 | tf_op jit(solution)/shard_map/psum | solution.py:102
  240.6 38.4 %reduce-scatter.4.cloned.1.call-done = f32[192,256]{1,0:T(8,128)} async-done(((f32[1536,256]{1,0:T(8,128)}), f32[192,256]{1,0:T(8,128)}) %reduce-scatter.4.cloned.1.call-update) | async-done | bytes 196624
  279.0 1.6 copy.132
  (120 shorter events, 33.9 us)
Async XLA Ops:
  7.2 1.2 copy-start
  7.2 5.1 %copy-start.2 = (bf16[1536,256]{1,0:T(8,128)(2,1)S(1)}, bf16[1536,256]{1,0:T(8,128)(2,1)}, u32[]{:S(2)}) copy-start(bf16[1536,256]{1,0:T(8,128)(2,1)} %param.14) | copy-start | bytes 2359300
  7.2 74.4 %all-gather.5.cloned.1.call-start = ((), (), s32[]{:S(2)}) async-start(), calls=%async_computation.2 | async-start | bytes 3932160 | tf_op jit(solution)/shard_map/all_gather | solution.py:9
  9.5 3.1 %copy-start.6 = (bf16[1,256,1536]{2,1,0:T(8,128)(2,1)S(1)}, bf16[1,256,1536]{2,1,0:T(8,128)(2,1)}, u32[]{:S(2)}) copy-start(bf16[1,256,1536]{2,1,0:T(8,128)(2,1)} %param.13) | copy-start | bytes 2359300
  10.9 0.6 copy-start.11
  12.6 0.7 copy-start.16
  15.2 146.9 %all-gather.7.cloned.1.call-start = ((), (), s32[]{:S(2)}) async-start(), calls=%async_computation.3 | async-start | bytes 3932160 | tf_op jit(solution)/shard_map/all_gather | solution.py:9
  16.7 80.5 %copy-start.1 = (bf16[1,256,1536]{1,2,0:T(8,128)(2,1)}, bf16[1,256,1536]{1,2,0:T(8,128)(2,1)S(1)}, u32[]{:S(2)}) copy-start(bf16[1,256,1536]{1,2,0:T(8,128)(2,1)S(1)} %copy.91) | copy-start | bytes 2359300
  99.8 140.8 %all-reduce.6.cloned.1.call-start = ((), (), s32[]{:S(2)}) async-start(), calls=%async_computation.1 | async-start | bytes 294912 | tf_op jit(solution)/shard_map/psum | solution.py:102
  107.2 7.4 %copy-start.17 = (pred[256,256]{1,0:T(8,128)(4,1)}, pred[256,256]{1,0:T(8,128)(4,1)S(1)}, u32[]{:S(2)}) copy-start(pred[256,256]{1,0:T(8,128)(4,1)S(1)} %iota_compare_fusion) | copy-start | bytes 196612
  108.0 6.6 %copy-start.20 = (f32[24,256]{1,0:T(8,128)}, f32[24,256]{1,0:T(8,128)S(1)}, u32[]{:S(2)}) copy-start(f32[24,256]{1,0:T(8,128)S(1)} %bitcast_add_fusion.8) | copy-start | bytes 73732
  108.2 6.4 %copy-start.13 = (f32[256,256]{1,0:T(8,128)}, f32[256,256]{1,0:T(8,128)S(1)}, u32[]{:S(2)}) copy-start(f32[256,256]{1,0:T(8,128)S(1)} %fusion.53) | copy-start | bytes 786436
  169.9 1.2 copy-start.24
  170.2 0.9 copy-start.4
  170.2 1.0 copy-start.9
  170.2 1.0 copy-start.10
  171.3 5.7 %copy-start.5 = (f32[256,256]{1,0:T(8,128)S(1)}, f32[256,256]{1,0:T(8,128)}, u32[]{:S(2)}) copy-start(f32[256,256]{1,0:T(8,128)} %get-tuple-element.353) | copy-start | bytes 786436
  174.0 3.4 %copy-start.7 = (f32[1,256,128]{1,2,0:T(8,128)S(1)}, f32[1,256,128]{1,2,0:T(8,128)}, u32[]{:S(2)}) copy-start(f32[1,256,128]{1,2,0:T(8,128)} %fusion.25) | copy-start | bytes 393220
  174.1 14.8 %copy-start.22 = (f32[24,2]{0,1:T(2,128)}, f32[24,2]{0,1:T(2,128)S(1)}, u32[]{:S(2)}) copy-start(f32[24,2]{0,1:T(2,128)S(1)} %slice_bitcast_fusion) | copy-start | bytes 580
  174.1 14.8 %copy-start.8 = (f32[24,256]{0,1:T(8,128)S(1)}, f32[24,256]{0,1:T(8,128)}, u32[]{:S(2)}) copy-start(f32[24,256]{0,1:T(8,128)} %copy.97) | copy-start | bytes 73732
  190.4 88.6 %reduce-scatter.4.cloned.1.call-start = ((), (), s32[]{:S(2)}) async-start(), calls=%async_computation.4 | async-start | bytes 1769472
  195.0 0.9 copy-start.12
  195.1 5.9 %copy-start.14 = (f32[256,256]{1,0:T(8,128)S(1)}, f32[256,256]{1,0:T(8,128)}, u32[]{:S(2)}) copy-start(f32[256,256]{1,0:T(8,128)} %copy-done.13) | copy-start | bytes 786436
  195.1 5.9 %copy-start.15 = (f32[256,24]{0,1:T(8,128)S(1)}, f32[256,24]{0,1:T(8,128)}, u32[]{:S(2)}) copy-start(f32[256,24]{0,1:T(8,128)} %copy.90) | copy-start | bytes 73732
  195.1 5.9 %copy-start.18 = (pred[256,256]{1,0:T(8,128)(4,1)S(1)}, pred[256,256]{1,0:T(8,128)(4,1)}, u32[]{:S(2)}) copy-start(pred[256,256]{1,0:T(8,128)(4,1)} %copy-done.17) | copy-start | bytes 196612
  195.1 5.9 %copy-start.19 = (f32[24,256]{1,0:T(8,128)S(1)}, f32[24,256]{1,0:T(8,128)}, u32[]{:S(2)}) copy-start(f32[24,256]{1,0:T(8,128)} %copy.95) | copy-start | bytes 73732
  195.1 5.9 %copy-start.21 = (f32[24,256]{1,0:T(8,128)S(1)}, f32[24,256]{1,0:T(8,128)}, u32[]{:S(2)}) copy-start(f32[24,256]{1,0:T(8,128)} %copy-done.20) | copy-start | bytes 73732
  207.0 2.4 copy-start.23
  207.0 2.6 copy-start.26
  207.0 2.6 copy-start.25
  207.0 21.1 %copy-start.3 = (bf16[1536,256]{1,0:T(8,128)(2,1)S(1)}, bf16[1536,256]{1,0:T(8,128)(2,1)}, u32[]{:S(2)}) copy-start(bf16[1536,256]{1,0:T(8,128)(2,1)} %param.14) | copy-start | bytes 2359300
Sparse Core Ops, SparseCore 0:
  15.3 66.1 all-gather.4
  99.9 62.1 all-gather.6
  190.6 49.9 all-reduce.5
  243.4 35.5 reduce-scatter.3
where the time goes:
time: 289 us; the launch traced here: 287 us
  waiting for transfers between devices  140 us (48%)
  blocking collectives  47.8 us (17%)
  matrix products  33.6 us (12%)
  local copies, waits for them, and re-layouts  30 us (10%)
  other arithmetic  21.3 us (7%)
  between operations  14.1 us (5%)
    all_gather x2, waiting for transfers between devices, prefix(): everything = jax.tree.map(lambda part: lax.all_gather(part, axis), shard)  90.5 us
    unnamed x5, waiting for transfers between devices  38.5 us
    psum x1, blocking collectives, on_device(): lax.psum((local_w_dt, jnp.sum(grad_pre, axis=0), jnp.sum(g_rate, axis=0)...  14.1 us
    all_gather x1, blocking collectives, prefix(): everything = jax.tree.map(lambda part: lax.all_gather(part, axis), shard)  12.8 us
    dot_general x2, matrix products, span_core(): inner = jnp.einsum('hts,shp->thp', mixing, values_in, precision=highest)  12.4 us
    psum x1, blocking collectives, on_device(): grad_proj = lax.psum(partial_proj, 'head').astype(jnp.bfloat16)  11.5 us
    psum x1, waiting for transfers between devices, on_device(): lax.psum((local_w_dt, jnp.sum(grad_pre, axis=0), jnp.sum(g_rate, axis=0)...  10.8 us
    unnamed x59, local copies, waits for them, and re-layouts  10.7 us
  transfers between devices with their start and end apart: 4, of which 4 were waited for; matrix products, arithmetic and copies ran while one was open for 14% of the time, Pallas kernels for 0%

commit v1 on v0

--- a/solution.py
+++ b/solution.py
@@ -100,7 +100,11 @@
     grad_values = g_x.reshape(seq_count, token_count, heads * head_size).astype(jnp.bfloat16)
     local_w_dt = jnp.einsum("td,th->dh", flat, grad_pre_b, preferred_element_type=jnp.float32)
     grad_w_dt, grad_dt_bias, grad_a_log = lax.psum(
-        (local_w_dt, jnp.sum(grad_pre, axis=0), jnp.sum(g_rate, axis=0) * rate), ("tm", "batch")
+        lax.psum(
+            (local_w_dt, jnp.sum(grad_pre, axis=0), jnp.sum(g_rate, axis=0) * rate),
+            axis_name="batch",
+        ),
+        axis_name="tm",
     )
     local_w_bc = jnp.einsum("td,tk->dk", flat, grad_proj, preferred_element_type=jnp.float32)
     grad_w_bc = lax.psum_scatter(local_w_bc, ("tm", "batch"), scatter_dimension=0, tiled=True)

time: 289 us -> 279 us (0.965)
  waiting for transfers between devices: 140 us -> 133 us
  local copies, waits for them, and re-layouts: 30 us -> 26.7 us
    psum x0 -> x1, blocking collectives: none -> 12.4 us  [on_device(): lax.psum(lax.psum((local_w_dt, jnp.sum(grad_pre, axis=0), jnp.sum(g_rate,...]
    psum x1, blocking collectives: 14.1 us -> 2.47 us  [on_device(): lax.psum((local_w_dt, jnp.sum(grad_pre, axis=0), jnp.sum(g_rate, axis=0)...]
    psum x1, waiting for transfers between devices: 10.8 us -> 5.25 us  [on_device(): lax.psum((local_w_dt, jnp.sum(grad_pre, axis=0), jnp.sum(g_rate, axis=0)...]
    unnamed x59 -> x57, local copies, waits for them, and re-layouts: 10.7 us -> 8.09 us
    unnamed x5 -> x6, waiting for transfers between devices: 38.5 us -> 37.2 us
  transfers between devices with their start and end apart: 4 -> 5, of which waited for: 4 -> 5; matrix products, arithmetic and copies ran while one was open for 14% -> 13% of each run, Pallas kernels for 0% -> 0%
where the time goes in v1:
time: 279 us; the launch traced here: 278 us
  waiting for transfers between devices  133 us (48%)
  blocking collectives  49.1 us (18%)
  matrix products  32.5 us (12%)
  local copies, waits for them, and re-layouts  26.7 us (10%)
  other arithmetic  21.3 us (8%)
  between operations  14.2 us (5%)
    all_gather x2, waiting for transfers between devices, prefix(): everything = jax.tree.map(lambda part: lax.all_gather(part, axis), shard)  90.5 us
    unnamed x6, waiting for transfers between devices  37.2 us
    all_gather x1, blocking collectives, prefix(): everything = jax.tree.map(lambda part: lax.all_gather(part, axis), shard)  12.8 us
    dot_general x2, matrix products, span_core(): inner = jnp.einsum('hts,shp->thp', mixing, values_in, precision=highest)  12.5 us
    psum x1, blocking collectives, on_device(): lax.psum(lax.psum((local_w_dt, jnp.sum(grad_pre, axis=0), jnp.sum(g_rate,...  12.4 us
    psum x1, blocking collectives, on_device(): grad_proj = lax.psum(partial_proj, 'head').astype(jnp.bfloat16)  11.5 us
    select_n x8, other arithmetic, turn(): return jax.tree.map(lambda a, b: jnp.where(reached, a, b), new, before)  10.4 us
    unnamed x57, local copies, waits for them, and re-layouts  8.09 us
  transfers between devices with their start and end apart: 5, of which 5 were waited for; matrix products, arithmetic and copies ran while one was open for 13% of the time, Pallas kernels for 0%

profile of v1, /device:TPU:0, one launch (start us, length us, event | category | flops | bytes accessed | tf_op | source)
XLA Modules:
  0.0 277.7 jit_solution(2344774273177045791)
XLA Ops:
  12.3 1.8 fusion.20
  15.7 12.8 %all_gather.24 = f32[4,1,24]{2,1,0:T(1,128)} all-gather(f32[1,1,24]{2,1,0:T(1,128)S(1)} %get-tuple-element.387), channel_id=1, replica_groups=mesh['groups'=2,'tm'=4,'head'=2,'batch'=2] {'tm'}, dimensions={0}, use_global_device_ids=true | all-gather | bytes 480 | tf_op jit(solution)/shard_map/all_gather | solution.py:9
  28.5 52.0 %all-gather.5.cloned.1.call-done = f32[96,64,128]{2,1,0:T(8,128)} async-done(((f32[24,64,128]{2,1,0:T(8,128)}), f32[96,64,128]{2,1,0:T(8,128)}) %all-gather.5.cloned.1.call-update) | async-done | bytes 3145744 | tf_op jit(solution)/shard_map/all_gather | solution.py:9
  80.5 7.8 %while.30 = (s32[]{:T(128)}, f32[1,24,64,128]{3,2,1,0:T(8,128)S(1)}, s32[]{:T(128)}, f32[4,1,24]{2,1,0:T(1,128)}, f32[4,1,24,64,128]{4,3,2,1,0:T(8,128)}, /*index=5*/s32[]{:T(128)}, s32[]{:T(128)}, s32[]{:T(128)}, s32[]{:T(128)}) while((s32[]{:T(128)}, f32[1,24,64,128]{3,2,1,0:T(8,128)S(1)}, s32[]{:T(128)}, f32[4,1,24]{2,1,0:T(1,128)}, ...), condition=%wide.region_3.4_spmd.clone, body=%wide.region_2.3_spmd.clone.sunk | while | flops 786440 | bytes 2359751 | solution.py:22
  88.4 2.5 fusion.18
  90.9 1.5 copy.111
  92.4 2.2 fusion.61
  94.6 1.6 copy.90
  96.2 2.5 fusion.16
  100.3 2.0 bitcast_multiply_fusion.1
  103.0 1.6 copy.112
  104.6 1.6 copy.95
  107.2 6.4 %fusion.7 = (f32[24,256]{1,0:T(8,128)}, f32[24,256]{1,0:T(8,128)}, f32[24,256]{1,0:T(8,128)}, f32[256,256]{1,0:T(8,128)}) fusion(f32[256,256]{1,0:T(8,128)S(1)} %fusion.53, f32[24,256]{1,0:T(8,128)} %copy.95, f32[24,256]{1,0:T(8,128)S(1)} %bitcast_add_fusion.8, pred[256,256]{1,0:T(8,128)(4,1)S(1)} %iota_compare_fusion, ...), kind=kOutput, calls=%fused_computation.14 | convolution fusion | flops 221689856 | bytes 2285568 | tf_op jit(solution)/shard_map/vmap(transpose(jvp(hts,shp->thp)))/dot_general | solution.py:34
  113.6 1.5 copy.100
  115.1 1.5 copy.99
  116.6 1.5 copy.97
  119.3 3.3 %fusion.25 = f32[1,256,128]{1,2,0:T(8,128)} fusion(f32[1,256,128]{1,2,0:T(8,128)S(1)} %convolution_bitcast_fusion.3, bf16[256,24,64]{0,2,1:T(8,128)(2,1)} %bitcast.249, f32[1,24,64,128]{3,2,1,0:T(8,128)S(1)} %get-tuple-element.232, f32[256,24]{0,1:T(8,128)} %copy.90), kind=kOutput, calls=%fused_computation.42 | convolution fusion | flops 604798976 | bytes 1859584 | tf_op jit(solution)/shard_map/vmap(transpose(jvp(sh,shp,sn->hpn)))/dot_general | solution.py:40
  122.5 38.5 %all-gather.7.cloned.1.call-done = f32[96,64,128]{2,1,0:T(8,128)} async-done(((f32[24,64,128]{2,1,0:T(8,128)}), f32[96,64,128]{2,1,0:T(8,128)}) %all-gather.7.cloned.1.call-update) | async-done | bytes 3145744 | tf_op jit(solution)/shard_map/all_gather | solution.py:9
  161.0 7.8 %while.31 = (s32[]{:T(128)}, f32[1,24,64,128]{3,2,1,0:T(8,128)S(1)}, s32[]{:T(128)}, f32[4,1,24]{2,1,0:T(1,128)}, f32[4,1,24,64,128]{4,3,2,1,0:T(8,128)}, /*index=5*/s32[]{:T(128)}, s32[]{:T(128)}) while((s32[]{:T(128)}, f32[1,24,64,128]{3,2,1,0:T(8,128)S(1)}, s32[]{:T(128)}, f32[4,1,24]{2,1,0:T(1,128)}, ...), condition=%wide.region_6.7_spmd.clone, body=%wide.region_5.6_spmd.clone.sunk | while | flops 786436 | bytes 2359689 | solution.py:22
  170.4 2.5 reduce-window.16
  173.1 2.9 %convolution_bitcast_fusion.2 = f32[256,128]{0,1:T(8,128)S(1)} fusion(f32[256,24,64]{0,2,1:T(8,128)} %bitcast.250, f32[1,24,64,128]{3,2,1,0:T(8,128)S(1)} %get-tuple-element.233), kind=kOutput, calls=%fused_computation.40 | convolution fusion | flops 603979776 | bytes 2490368 | tf_op jit(solution)/shard_map/vmap(transpose(jvp(tn,hpn->thp)))/dot_general | solution.py:35
  178.0 11.5 %all-reduce.11 = bf16[256,256]{0,1:T(8,128)(2,1)S(1)} all-reduce(f32[256,256]{0,1:T(8,128)S(1)} %maximum_bitcast_fusion), channel_id=1, replica_groups=mesh['groups'=2,'tm'=4,'head'=2,'batch'=2] {'head'}, use_global_device_ids=true, to_apply=%region_7.8 | all-reduce | flops 65536 | bytes 393216 | tf_op jit(solution)/shard_map/psum | solution.py:90
  189.5 5.2 %all-reduce.8.cloned.1.call-done = f32[1536,24]{0,1:T(8,128)} async-done(((f32[1536,24]{0,1:T(8,128)}), f32[1536,24]{0,1:T(8,128)}) %all-reduce.8.cloned.1.call-update) | async-done | bytes 147472 | tf_op jit(solution)/shard_map/psum | solution.py:103
  195.2 1.6 copy.113
  196.8 5.5 %all_gather.30 = bf16[1536,48]{0,1:T(8,128)(2,1)S(1)} all-gather(bf16[1536,24]{0,1:T(8,128)(2,1)} %param.15), channel_id=1, replica_groups=mesh['groups'=2,'tm'=4,'head'=2,'batch'=2] {'head'}, dimensions={1}, use_global_device_ids=true | all-gather | bytes 221184 | tf_op jit(solution)/shard_map/all_gather | solution.py:96
  202.4 6.1 %fusion.19 = bf16[1,256,24,64]{1,3,2,0:T(8,128)(2,1)} fusion(f32[24,64,256]{2,1,0:T(8,128)S(1)} %copy-done.5, bf16[24,64,256]{2,1,0:T(8,128)(2,1)S(1)} %bitcast.245, f32[256,256]{1,0:T(8,128)} %copy-done.17, f32[24,256]{1,0:T(8,128)} %copy.95, f32[24,256]{1,0:T(8,128)} %copy-done.20, pred[256,256]{1,0:T(8,128)(4,1)} %copy-done.19, f32[256,24]{0,1:T(8,128)} %copy.90), kind=kOutput, calls=%fused_computation.32 | convolution fusion | flops 1215430656 | bytes 3547136 | tf_op jit(solution)/shard_map/vmap(transpose(jvp(hts,shp->thp)))/dot_general | solution.py:34
  208.5 2.4 copy.104
  211.1 2.5 all-reduce.3
  213.6 12.4 %all-reduce.2 = (f32[24]{0:T(128)}, f32[24]{0:T(128)}) all-reduce(f32[24]{0:T(128)S(1)} %get-tuple-element.376, f32[24]{0:T(128)S(1)} %get-tuple-element.377), channel_id=1, replica_groups=mesh['groups'=2,'tm'=4,'head'=2,'batch'=2] {'tm'}, use_global_device_ids=true, to_apply=%region_21.22 | all-reduce | flops 48 | bytes 384 | tf_op jit(solution)/shard_map/psum | solution.py:102
  226.0 4.4 %all_gather.29 = bf16[256,48]{0,1:T(8,128)(2,1)S(1)} all-gather(bf16[256,24]{0,1:T(8,128)(2,1)S(1)} %copy.103), channel_id=1, replica_groups=mesh['groups'=2,'tm'=4,'head'=2,'batch'=2] {'head'}, dimensions={1}, use_global_device_ids=true | all-gather | bytes 36864 | tf_op jit(solution)/shard_map/all_gather | solution.py:95
  232.4 37.1 %reduce-scatter.4.cloned.1.call-done = f32[192,256]{1,0:T(8,128)} async-done(((f32[1536,256]{1,0:T(8,128)}), f32[192,256]{1,0:T(8,128)}) %reduce-scatter.4.cloned.1.call-update) | async-done | bytes 196624
  269.6 1.6 copy.133
  (122 shorter events, 32.9 us)
Async XLA Ops:
  7.2 1.2 copy-start
  7.2 4.5 %copy-start.2 = (bf16[1536,256]{1,0:T(8,128)(2,1)S(1)}, bf16[1536,256]{1,0:T(8,128)(2,1)}, u32[]{:S(2)}) copy-start(bf16[1536,256]{1,0:T(8,128)(2,1)} %param.14) | copy-start | bytes 2359300
  7.2 73.3 %all-gather.5.cloned.1.call-start = ((), (), s32[]{:S(2)}) async-start(), calls=%async_computation.3 | async-start | bytes 3932160 | tf_op jit(solution)/shard_map/all_gather | solution.py:9
  9.5 2.5 copy-start.9
  10.9 0.6 copy-start.16
  11.6 0.7 copy-start.18
  14.2 146.9 %all-gather.7.cloned.1.call-start = ((), (), s32[]{:S(2)}) async-start(), calls=%async_computation.4 | async-start | bytes 3932160 | tf_op jit(solution)/shard_map/all_gather | solution.py:9
  15.6 80.5 %copy-start.1 = (bf16[1,256,1536]{1,2,0:T(8,128)(2,1)}, bf16[1,256,1536]{1,2,0:T(8,128)(2,1)S(1)}, u32[]{:S(2)}) copy-start(bf16[1,256,1536]{1,2,0:T(8,128)(2,1)S(1)} %copy.91) | copy-start | bytes 2359300
  98.7 96.0 %all-reduce.8.cloned.1.call-start = ((), (), s32[]{:S(2)}) async-start(), calls=%async_computation.1 | async-start | bytes 294912 | tf_op jit(solution)/shard_map/psum | solution.py:103
  106.2 7.4 %copy-start.19 = (pred[256,256]{1,0:T(8,128)(4,1)}, pred[256,256]{1,0:T(8,128)(4,1)S(1)}, u32[]{:S(2)}) copy-start(pred[256,256]{1,0:T(8,128)(4,1)S(1)} %iota_compare_fusion) | copy-start | bytes 196612
  107.0 6.6 %copy-start.20 = (f32[24,256]{1,0:T(8,128)}, f32[24,256]{1,0:T(8,128)S(1)}, u32[]{:S(2)}) copy-start(f32[24,256]{1,0:T(8,128)S(1)} %bitcast_add_fusion.8) | copy-start | bytes 73732
  107.2 6.4 %copy-start.17 = (f32[256,256]{1,0:T(8,128)}, f32[256,256]{1,0:T(8,128)S(1)}, u32[]{:S(2)}) copy-start(f32[256,256]{1,0:T(8,128)S(1)} %fusion.53) | copy-start | bytes 786436
  168.8 1.2 copy-start.23
  169.1 0.9 copy-start.4
  169.1 1.0 copy-start.14
  169.1 1.0 copy-start.15
  170.3 5.8 %copy-start.8 = (f32[256,256]{1,0:T(8,128)S(1)}, f32[256,256]{1,0:T(8,128)}, u32[]{:S(2)}) copy-start(f32[256,256]{1,0:T(8,128)} %get-tuple-element.353) | copy-start | bytes 786436
  173.0 3.4 %copy-start.6 = (f32[1,24,2,128]{1,3,2,0:T(8,128)}, f32[1,24,2,128]{1,3,2,0:T(8,128)S(1)}, u32[]{:S(2)}) copy-start(f32[1,24,2,128]{1,3,2,0:T(8,128)S(1)} %copy.102) | copy-start | bytes 73732
  173.0 3.4 %copy-start.12 = (f32[1,256,128]{1,2,0:T(8,128)S(1)}, f32[1,256,128]{1,2,0:T(8,128)}, u32[]{:S(2)}) copy-start(f32[1,256,128]{1,2,0:T(8,128)} %fusion.25) | copy-start | bytes 393220
  173.1 3.3 %copy-start.21 = (f32[24,2]{0,1:T(2,128)}, f32[24,2]{0,1:T(2,128)S(1)}, u32[]{:S(2)}) copy-start(f32[24,2]{0,1:T(2,128)S(1)} %slice_bitcast_fusion) | copy-start | bytes 580
  173.1 3.3 %copy-start.13 = (f32[24,256]{0,1:T(8,128)S(1)}, f32[24,256]{0,1:T(8,128)}, u32[]{:S(2)}) copy-start(f32[24,256]{0,1:T(8,128)} %copy.97) | copy-start | bytes 73732
  177.0 0.9 copy-start.10
  178.0 54.5 %all-reduce.10.cloned.1.call-start = ((), (), s32[]{:S(2)}) async-start(), calls=%async_computation.2 | async-start | bytes 294912 | tf_op jit(solution)/shard_map/psum | solution.py:102
  194.8 74.8 %reduce-scatter.4.cloned.1.call-start = ((), (), s32[]{:S(2)}) async-start(), calls=%async_computation.5 | async-start | bytes 1769472
  196.8 5.5 %copy-start.5 = (f32[24,64,256]{2,1,0:T(8,128)S(1)}, f32[24,64,256]{2,1,0:T(8,128)}, u32[]{:S(2)}) copy-start(f32[24,64,256]{2,1,0:T(8,128)} %get-tuple-element.389) | copy-start | bytes 4718596
  208.4 2.4 copy-start.7
  208.4 2.4 copy-start.22
  208.4 2.6 copy-start.11
  208.4 2.6 copy-start.25
  208.5 2.6 copy-start.24
  208.5 21.9 %copy-start.3 = (bf16[1536,256]{1,0:T(8,128)(2,1)S(1)}, bf16[1536,256]{1,0:T(8,128)(2,1)}, u32[]{:S(2)}) copy-start(bf16[1536,256]{1,0:T(8,128)(2,1)} %param.14) | copy-start | bytes 2359300
Sparse Core Ops, SparseCore 0:
  14.3 66.1 all-gather.4
  98.8 62.1 all-gather.6
  178.1 16.6 all-reduce.7
  196.9 35.4 all-reduce.9
  235.3 34.2 reduce-scatter.3
